TPU v7x, 512 devices: a whole 4x4x16 slice. The times are simulated.
512 devices in a mesh: dp: 128 (over x, z, core), mp: 4 (over y).
Axes of the slice: x: 4, y: 4, z: 16, core: 2. Of those that a mesh axis runs over, the one named last changes fastest.
Arguments:
- x_in: bfloat16 [16384, 1024], P('dp', 'mp'), may hold values from -90 to 90
- gain: float32 [1024], replicated, may hold values from 0.25 to 1.75
- w_in: bfloat16 [1024, 4096], P('mp'), may hold values from -0.5 to 0.5
- w_out: bfloat16 [1024, 4096], P('mp'), may hold values from -0.1875 to 0.1875
- grad_out: bfloat16 [16384, 1024], P('dp', 'mp'), may hold values from -6 to 6
- block_cols: int32 [4, 256], P('mp'), may hold values from 0 to 127, as said below
- slots: int32 [4, 256], P('mp'), may hold values from 0 to 511, as said below
Outputs:
- branch: bfloat16 [16384, 1024], P('dp', 'mp')
- grad_normed: bfloat16 [16384, 1024], P('dp', 'mp')
- owned_grad: float32 [4, 512, 4096], P('mp', 'dp')
Inputs may be any that keep to these rules, and one draw needn't show every extreme that they name: Within one row of block_cols, the 16 entries k with the same k // 16 are distinct. The entries of one row of slots are distinct; slot s lies on index s // 4 of dp. In each row every index of dp holds at most 4 slots that are named, and some index holds exactly 4.
All inputs are finite; a program needn't handle non-finite values.
Results may differ from a plain program's by a relative error of at most 0.0062.
Values may be sent and summed in bfloat16 or wider, within the bound.
A program may use at most 128 MiB of HBM per device.

v0:
```python
import functools
import math

import jax
import jax.numpy as jnp
from jax import lax
from jax.experimental import pallas as pl
from jax.experimental.pallas import tpu as pltpu
from jax.sharding import PartitionSpec as P

BLK = 64
NRB = 16
KR = 16
NCB = 128
TOK = 128
NX = 4
NZ = 16
NMP = 4
FWD = NZ // 2
BWD = NZ - 1 - FWD

norm_eps = 1e-06
tanh_coef = 0.7978845608028654
f32 = jnp.float32
bf16 = jnp.bfloat16
MESH = pl.DeviceIdType.MESH
NT = (((1,), (1,)), ((), ()))
TN = (((0,), (0,)), ((), ()))


def signal_all(peers):
    barrier = pltpu.get_barrier_semaphore()
    for peer in peers:
        pl.semaphore_signal(barrier, inc=1, device_id=peer, device_id_type=MESH)
    pl.semaphore_wait(barrier, len(peers))


def remote(src, dst, send, recv, peer):
    return pltpu.make_async_remote_copy(
        src_ref=src, dst_ref=dst, send_sem=send, recv_sem=recv,
        device_id=peer, device_id_type=MESH,
    )


def gather_kernel(x_ref, g_ref, xo_ref, go_ref, send, recv):
    me = lax.axis_index("mp")
    peers = [{"mp": lax.rem(me + i, NMP)} for i in range(1, NMP)]
    signal_all(peers)
    copies = []
    for i, peer in enumerate(peers):
        copies.append(remote(x_ref, xo_ref.at[me], send.at[0, i], recv.at[0, i], peer))
        copies.append(remote(g_ref, go_ref.at[me], send.at[1, i], recv.at[1, i], peer))
    for copy in copies:
        copy.start()
    xo_ref[me] = x_ref[...]
    go_ref[me] = g_ref[...]
    for copy in copies:
        copy.wait()


def gather_inputs(x_in, grad_out):
    whole = jax.ShapeDtypeStruct((NMP, TOK, x_in.shape[1]), bf16)
    vmem = pl.BlockSpec(memory_space=pltpu.VMEM)
    return pl.pallas_call(
        gather_kernel,
        out_shape=(whole, whole),
        in_specs=[vmem, vmem],
        out_specs=(vmem, vmem),
        scratch_shapes=[
            pltpu.SemaphoreType.DMA((2, NMP - 1)),
            pltpu.SemaphoreType.DMA((2, NMP - 1)),
        ],
        compiler_params=pltpu.CompilerParams(collective_id=0, has_side_effects=True),
        name="gather_inputs",
    )(x_in, grad_out)


def compute_kernel(scale, cols, slots, x_ref, g_ref, gain_ref, w_ref,
                   out_ref, branch_ref, gn_ref,
                   normed, pre, gact, act, gpre, parts, gath, halves, brt, gnt):
    squares = jnp.zeros((TOK, 1), f32)
    for p in range(NMP):
        xf = x_ref[p].astype(f32)
        squares += jnp.sum(xf * xf, axis=-1, keepdims=True)
    inv_rms = lax.rsqrt(squares / (NRB * BLK) + norm_eps)
    for p in range(NMP):
        normed[p] = (x_ref[p].astype(f32) * inv_rms * gain_ref[p]).astype(bf16)

    @pl.loop(0, NCB)
    def _(i):
        rows = pl.ds(pl.multiple_of(i * BLK, BLK), BLK)
        pre[rows, :] = jnp.zeros((BLK, TOK), f32)
        gact[rows, :] = jnp.zeros((BLK, TOK), f32)
        for j in range(4):
            out_ref[i * 4 + j] = jnp.zeros((BLK // 2, 2 * BLK), bf16)

    blank = jnp.zeros((TOK, BLK), bf16)

    def stacked(top, bottom):
        return jnp.concatenate([
            jnp.concatenate([top, blank], axis=1),
            jnp.concatenate([blank, bottom], axis=1),
        ], axis=0)

    @pl.loop(0, NMP)
    def _(p):
        for q in range(NRB // NMP):
            r = p * (NRB // NMP) + q
            lanes = slice(q * BLK, (q + 1) * BLK)
            both = stacked(normed[p, :, lanes], g_ref[p, :, lanes])
            rows = pl.ds(pl.multiple_of(r * KR * BLK, KR * BLK), KR * BLK)
            parts[...] = lax.dot_general(w_ref[rows, :], both, NT, preferred_element_type=f32)
            for k in range(KR):
                at = pl.ds(pl.multiple_of(cols[0, r * KR + k] * BLK, BLK), BLK)
                pre[at, :] += parts[k * BLK:(k + 1) * BLK, :TOK]
                gact[at, :] += parts[k * BLK:(k + 1) * BLK, TOK:]

    @pl.loop(0, NCB)
    def _(i):
        rows = pl.ds(pl.multiple_of(i * BLK, BLK), BLK)
        v = pre[rows, :]
        square = v * v
        th = jnp.tanh(tanh_coef * (v + 0.044715 * (square * v)))
        half = 0.5 * v
        act[rows, :] = (half * (1.0 + th)).astype(bf16)
        inner = tanh_coef * (1.0 + 0.134145 * square)
        slope = 0.5 * (1.0 + th) + half * (1.0 - th * th) * inner
        gpre[rows, :] = (gact[rows, :] * slope).astype(bf16)

    @pl.loop(0, NMP)
    def _(p):
        for q in range(NRB // NMP):
            r = p * (NRB // NMP) + q
            lanes = slice(q * BLK, (q + 1) * BLK)
            n_r = normed[p, :, lanes]
            for k in range(KR):
                at = pl.ds(pl.multiple_of(cols[0, r * KR + k] * BLK, BLK), BLK)
                block = gpre[at, :]
                gath[k * BLK:(k + 1) * BLK, :TOK] = block
                gath[k * BLK:(k + 1) * BLK, TOK:] = act[at, :]
                halves[k * 32:(k + 1) * 32, :TOK] = block[:32]
                halves[k * 32:(k + 1) * 32, TOK:] = block[32:]
            rows = pl.ds(pl.multiple_of(r * KR * BLK, KR * BLK), KR * BLK)
            sums = lax.dot_general(w_ref[rows, :], gath[...], TN, preferred_element_type=f32)
            at = pl.ds(pl.multiple_of(r * BLK, BLK), BLK)
            gnt[at, :] = sums[:BLK, :TOK]
            brt[at, :] = sums[BLK:, TOK:]
            grads = jnp.dot(halves[...], stacked(n_r, n_r), preferred_element_type=f32)
            grads = (grads * scale).astype(bf16)
            for k in range(KR):
                s = slots[0, r * KR + k]
                x, z, core, j = s // 128, (s // 8) % NZ, (s // 4) % 2, s % 4
                out_ref[((core * NZ + z) * NX + x) * 4 + j] = grads[k * 32:(k + 1) * 32]

    for p in range(NMP):
        rows = slice(p * 256, (p + 1) * 256)
        gn_ref[p] = gnt[rows, :].T.astype(bf16)
        branch_ref[p] = brt[rows, :].T.astype(bf16)


def compute(cols, slots, whole_x, whole_grad, gain, weights):
    vmem = pl.BlockSpec(memory_space=pltpu.VMEM)
    smem = pl.BlockSpec(memory_space=pltpu.SMEM)
    feats = jax.ShapeDtypeStruct((NMP, TOK, 256), bf16)
    scale = 1.0 / math.sqrt(TOK * 2 * NX * NZ)
    return pl.pallas_call(
        functools.partial(compute_kernel, scale),
        out_shape=(jax.ShapeDtypeStruct((512, BLK // 2, 2 * BLK), bf16), feats, feats),
        in_specs=[smem, smem, vmem, vmem, vmem, vmem],
        out_specs=(vmem, vmem, vmem),
        scratch_shapes=[
            pltpu.VMEM((NMP, TOK, 256), bf16),
            pltpu.VMEM((NCB * BLK, TOK), f32),
            pltpu.VMEM((NCB * BLK, TOK), f32),
            pltpu.VMEM((NCB * BLK, TOK), bf16),
            pltpu.VMEM((NCB * BLK, TOK), bf16),
            pltpu.VMEM((KR * BLK, 2 * TOK), f32),
            pltpu.VMEM((KR * BLK, 2 * TOK), bf16),
            pltpu.VMEM((KR * BLK // 2, 2 * TOK), bf16),
            pltpu.VMEM((NRB * BLK, TOK), f32),
            pltpu.VMEM((NRB * BLK, TOK), f32),
        ],
        compiler_params=pltpu.CompilerParams(vmem_limit_bytes=48 << 20),
        name="local_compute",
    )(cols, slots, whole_x, whole_grad, gain, weights)


def reduce_kernel(src, br_src, gn_src, owned, br_out, gn_out,
                  from_core, f_send, f_recv, b_send, b_recv, x_send, x_recv, m_recv,
                  core_ss, core_rs, f_ss, f_rs, b_ss, b_rs, x_ss, x_rs, m_ss, m_rs):
    dp, mp = lax.axis_index("dp"), lax.axis_index("mp")
    core = lax.rem(dp, 2)
    z = lax.rem(dp // 2, NZ)
    x = dp // (2 * NZ)

    def at(xx, zz, cc):
        return {"dp": (xx * NZ + zz) * 2 + cc}

    partner = at(x, z, 1 - core)
    ahead = at(x, lax.rem(z + 1, NZ), core)
    behind = at(x, lax.rem(z + NZ - 1, NZ), core)
    x_peers = [at(lax.rem(x + i, NX), z, core) for i in range(1, NX)]
    m_peers = [{"mp": lax.rem(mp + i, NMP)} for i in range(1, NMP)]
    signal_all([partner, ahead, behind] + x_peers + m_peers)

    def f_dest(s):
        return lax.rem(z + FWD - s, NZ)

    def b_dest(s):
        return lax.rem(z + NZ - BWD + s, NZ)

    core_copies = {}

    def core_copy(d):
        return remote(src.at[1 - core, d], from_core.at[d], core_ss.at[d], core_rs.at[d], partner)

    @pl.loop(0, FWD)
    def _(s):
        core_copy(f_dest(s)).start()

        @pl.when(s < BWD)
        def _():
            core_copy(b_dest(s)).start()

    core_copy(z).start()
    mp_copies = []
    for i, peer in enumerate(m_peers):
        to = lax.rem(mp + i + 1, NMP)
        mp_copies.append(remote(br_src.at[to], m_recv.at[0, i], m_ss.at[0, i], m_rs.at[0, i], peer))
        mp_copies.append(remote(gn_src.at[to], m_recv.at[1, i], m_ss.at[1, i], m_rs.at[1, i], peer))
    for copy in mp_copies:
        copy.start()

    def f_copy(s, q):
        return remote(f_send.at[s, q], f_recv.at[s, q], f_ss.at[s, q], f_rs.at[s, q], ahead)

    def b_copy(s, q):
        return remote(b_send.at[s, q], b_recv.at[s, q], b_ss.at[s, q], b_rs.at[s, q], behind)

    def pair(d, q):
        return src[core, d, q].astype(f32) + from_core[d, q].astype(f32)

    core_copy(f_dest(0)).wait_recv()
    for q in range(NX):
        f_send[0, q] = pair(f_dest(0), q).astype(bf16)
        f_copy(0, q).start()
    core_copy(b_dest(0)).wait_recv()
    for q in range(NX):
        b_send[0, q] = pair(b_dest(0), q).astype(bf16)
        b_copy(0, q).start()

    @pl.loop(1, FWD)
    def _(s):
        core_copy(f_dest(s)).wait_recv()

        @pl.when(s < BWD)
        def _():
            core_copy(b_dest(s)).wait_recv()

        for q in range(NX):
            f_copy(s - 1, q).wait_recv()
            f_send[s, q] = (pair(f_dest(s), q) + f_recv[s - 1, q].astype(f32)).astype(bf16)
            f_copy(s, q).start()

            @pl.when(s < BWD)
            def _():
                b_copy(s - 1, q).wait_recv()
                b_send[s, q] = (pair(b_dest(s), q) + b_recv[s - 1, q].astype(f32)).astype(bf16)
                b_copy(s, q).start()

    for o, (out, own_part) in enumerate(((br_out, br_src), (gn_out, gn_src))):
        total = own_part[mp].astype(f32)
        for i in range(NMP - 1):
            mp_copies[2 * i + o].wait_recv()
            total += m_recv[o, i].astype(f32)
        out[...] = total.astype(bf16)

    core_copy(z).wait_recv()
    for q in range(NX):
        b_copy(BWD - 1, q).wait_recv()
    for q in range(NX):
        f_copy(FWD - 1, q).wait_recv()

    def whole(q):
        return pair(z, q) + f_recv[FWD - 1, q].astype(f32) + b_recv[BWD - 1, q].astype(f32)

    x_copies = []
    for i, peer in enumerate(x_peers):
        x_send[i] = whole(lax.rem(x + i + 1, NX)).astype(bf16)
        copy = remote(x_send.at[i], x_recv.at[i], x_ss.at[i], x_rs.at[i], peer)
        copy.start()
        x_copies.append(copy)
    total = whole(x)
    for i in range(NX - 1):
        x_copies[i].wait_recv()
        total += x_recv[i].astype(f32)
    owned[...] = total

    for copy in x_copies + mp_copies:
        copy.wait_send()

    @pl.loop(0, NZ)
    def _(d):
        core_copy(d).wait_send()

    @pl.loop(0, FWD)
    def _(s):
        for q in range(NX):
            f_copy(s, q).wait_send()

            @pl.when(s < BWD)
            def _():
                b_copy(s, q).wait_send()


def reduce_all(outgoing, branch_parts, gn_parts):
    vmem = pl.BlockSpec(memory_space=pltpu.VMEM)
    dma = pltpu.SemaphoreType.DMA
    chunk = (NX, TOK, 128)
    feats = jax.ShapeDtypeStruct((TOK, 256), bf16)
    return pl.pallas_call(
        reduce_kernel,
        out_shape=(jax.ShapeDtypeStruct((TOK, 128), f32), feats, feats),
        in_specs=[vmem, vmem, vmem],
        out_specs=(vmem, vmem, vmem),
        scratch_shapes=[
            pltpu.VMEM((NZ,) + chunk, bf16),
            pltpu.VMEM((FWD,) + chunk, bf16),
            pltpu.VMEM((FWD,) + chunk, bf16),
            pltpu.VMEM((BWD,) + chunk, bf16),
            pltpu.VMEM((BWD,) + chunk, bf16),
            pltpu.VMEM((NX - 1, TOK, 128), bf16),
            pltpu.VMEM((NX - 1, TOK, 128), bf16),
            pltpu.VMEM((2, NMP - 1, TOK, 256), bf16),
            dma((NZ,)), dma((NZ,)),
            dma((FWD, NX)), dma((FWD, NX)),
            dma((BWD, NX)), dma((BWD, NX)),
            dma((NX - 1,)), dma((NX - 1,)),
            dma((2, NMP - 1)), dma((2, NMP - 1)),
        ],
        compiler_params=pltpu.CompilerParams(
            collective_id=1, has_side_effects=True, vmem_limit_bytes=40 << 20),
        name="reduce_all",
    )(outgoing.reshape(2, NZ, NX, TOK, 128), branch_parts, gn_parts)


def body(x_in, gain, w_in, w_out, grad_out, block_cols, slots):
    whole_x, whole_grad = gather_inputs(x_in, grad_out)
    weights = jnp.concatenate([
        w_in.reshape(-1, BLK, BLK).transpose(0, 2, 1),
        w_out.reshape(-1, BLK, BLK),
    ], axis=-1).reshape(-1, 2 * BLK)
    outgoing, branch_parts, gn_parts = compute(
        block_cols, slots, whole_x, whole_grad, gain.reshape(NMP, 1, 256), weights)
    owned, branch, grad_normed = reduce_all(outgoing, branch_parts, gn_parts)
    owned = owned.reshape(4, BLK // 2, 2, BLK).transpose(0, 2, 1, 3).reshape(1, 4, BLK * BLK)
    return (branch, grad_normed, owned)


def solution(mesh):
    placed = (
        P("dp", "mp"),
        P(),
        P("mp", None),
        P("mp", None),
        P("dp", "mp"),
        P("mp", None),
        P("mp", None),
    )
    return jax.shard_map(
        body,
        mesh=mesh,
        in_specs=placed,
        out_specs=(P("dp", "mp"), P("dp", "mp"), P("mp", "dp", None)),
        check_vma=False,
    )
```

profile of v0, /device:TPU:8, one launch (start us, length us, event | category | flops | bytes accessed | tf_op | source)
XLA Modules:
  0.0 104.8 jit_solution(1534365783078914748)
XLA Ops:
  0.6 14.1 %gather_inputs.1 = (bf16[4,128,256]{2,1,0:T(8,128)(2,1)}, bf16[4,128,256]{2,1,0:T(8,128)(2,1)}) custom-call(bf16[128,256]{1,0:T(8,128)(2,1)} %x_ref.1, bf16[128,256]{1,0:T(8,128)(2,1)} %g_ref.1), custom_call_target="tpu_custom_call" | custom-call | tf_op jit(solution)/shard_map/gather_inputs/pallas_call | solution.py:64
  14.7 3.3 %copy.12 = bf16[256,4096]{0,1:T(8,128)(2,1)S(1)} copy(bf16[256,4096]{1,0:T(8,128)(2,1)} %param.9) | data formatting | bytes 4194304 | tf_op args[2]
  18.0 8.0 %copy.13 = bf16[256,64,64]{2,1,0:T(8,128)(2,1)} copy(bf16[256,64,64]{0,1,2:T(8,128)(2,1)S(1)} %bitcast.12) | data formatting | bytes 4194304 | tf_op jit(solution)/shard_map/transpose | solution.py:350
  26.1 6.9 %concatenate.9 = bf16[16384,64]{1,0:T(8,128)(2,1)} reshape(bf16[256,4096]{1,0:T(8,128)(2,1)} %param.10) | data formatting | bytes 4194304 | tf_op jit(solution)/shard_map/concatenate | solution.py:349
  33.0 0.0 copy-start
  33.0 0.0 copy-start.1
  33.0 0.0 copy-start.2
  33.0 0.0 copy-start.3
  33.0 0.0 copy-start.4
  33.0 6.0 %pad_maximum_fusion.w_ref = bf16[16384,128]{1,0:T(8,128)(2,1)} fusion(bf16[16384,64]{1,0:T(8,128)(2,1)} %concatenate.9, bf16[16384,64]{1,0:T(8,128)(2,1)} %bitcast.11), kind=kLoop, calls=%fused_computation | loop fusion | flops 8388608 | bytes 8388608 | tf_op jit(solution)/shard_map/concatenate | solution.py:349
  39.0 0.0 copy-done
  39.0 0.0 copy-done.1
  39.0 0.0 copy-done.2
  39.0 0.0 copy-done.3
  39.0 0.0 copy-done.4
  39.0 18.0 %local_compute.1 = (bf16[512,32,128]{2,1,0:T(8,128)(2,1)S(1)}, bf16[4,128,256]{2,1,0:T(8,128)(2,1)S(1)}, bf16[4,128,256]{2,1,0:T(8,128)(2,1)S(1)}) custom-call(s32[1,256]{1,0:T(1,128)S(1)} %copy-done.3, s32[1,256]{1,0:T(1,128)S(1)} %copy-done.4, bf16[4,128,256]{2,1,0:T(8,128)(2,1)S(1)} %copy-done, bf16[4,128,256]{2,1,0:T(8,128)(2,1)S(1)} %copy-done.1, ...), custom_call_target="tpu_custom_call" | custom-call | tf_op jit(solution)/shard_map/local_compute/pallas_call | solution.py:166
  57.0 45.6 %reduce_all.1 = (f32[128,128]{1,0:T(8,128)S(1)}, bf16[128,256]{1,0:T(8,128)(2,1)S(1)}, bf16[128,256]{1,0:T(8,128)(2,1)S(1)}) custom-call(bf16[2,16,4,128,128]{4,3,2,1,0:T(8,128)(2,1)S(1)} %bitcast.9, bf16[4,128,256]{2,1,0:T(8,128)(2,1)S(1)} %get-tuple-element.14.br_src, bf16[4,128,256]{2,1,0:T(8,128)(2,1)S(1)} %get-tuple-element.15.gn_src), custom_call_target="tpu_custom_call" | custom-call | tf_op jit(solution)/shard_map/reduce_all/pallas_call | solution.py:321
  102.6 0.1 reshape.29
  102.8 0.7 reshape.30
  103.5 0.6 copy.17
  104.2 0.6 copy.18
  (1 shorter events, 0.0 us)
Async XLA Ops:
  33.0 6.0 %copy-start = (bf16[4,128,256]{2,1,0:T(8,128)(2,1)S(1)}, bf16[4,128,256]{2,1,0:T(8,128)(2,1)}, u32[]{:S(2)}) copy-start(bf16[4,128,256]{2,1,0:T(8,128)(2,1)} %get-tuple-element.11.x_ref) | copy-start | bytes 786436
  33.0 6.0 %copy-start.1 = (bf16[4,128,256]{2,1,0:T(8,128)(2,1)S(1)}, bf16[4,128,256]{2,1,0:T(8,128)(2,1)}, u32[]{:S(2)}) copy-start(bf16[4,128,256]{2,1,0:T(8,128)(2,1)} %get-tuple-element.12.g_ref) | copy-start | bytes 786436
  33.0 6.0 %copy-start.2 = (f32[1024]{0:T(1024)S(1)}, f32[1024]{0:T(1024)}, u32[]{:S(2)}) copy-start(f32[1024]{0:T(1024)} %param.8) | copy-start | bytes 12292
  33.0 6.0 %copy-start.3 = (s32[1,256]{1,0:T(1,128)S(1)}, s32[1,256]{1,0:T(1,128)}, u32[]{:S(2)}) copy-start(s32[1,256]{1,0:T(1,128)} %cols.1) | copy-start | bytes 3076
  33.0 6.0 %copy-start.4 = (s32[1,256]{1,0:T(1,128)S(1)}, s32[1,256]{1,0:T(1,128)}, u32[]{:S(2)}) copy-start(s32[1,256]{1,0:T(1,128)} %slots.1) | copy-start | bytes 3076
where the time goes:
time: 105 us
  Pallas kernels  77.7 us (74%)
  local copies, waits for them, and re-layouts  20.4 us (19%)
  other arithmetic  5.98 us (6%)
    pallas_call x1, Pallas kernels, reduce_all(): pl.pallas_call(reduce_kernel, out_shape=(jax.ShapeDtypeStruct((TOK, 128),...  45.6 us
    pallas_call x1, Pallas kernels, compute(): pl.pallas_call(functools.partial(compute_kernel, scale), out_shape=(jax.S...  18 us
    pallas_call x1, Pallas kernels, gather_inputs(): pl.pallas_call(gather_kernel, out_shape=(whole, whole), in_specs=[vmem, v...  14.1 us
    transpose x1, local copies, waits for them, and re-layouts, body(): w_in.reshape(-1, BLK, BLK).transpose(0, 2, 1)  8.05 us
    concatenate x1, local copies, waits for them, and re-layouts, body(): jnp.concatenate([w_in.reshape(-1, BLK, BLK).transpose(0, 2, 1), w_out.res...  6.92 us
    concatenate x1, other arithmetic, body(): jnp.concatenate([w_in.reshape(-1, BLK, BLK).transpose(0, 2, 1), w_out.res...  5.98 us
    unnamed x13, local copies, waits for them, and re-layouts  4.56 us

commit v1 on v0

--- a/solution.py
+++ b/solution.py
@@ -18,6 +18,7 @@
 NMP = 4
 FWD = NZ // 2
 BWD = NZ - 1 - FWD
+RELAY_AT = 4
 
 norm_eps = 1e-06
 tanh_coef = 0.7978845608028654
@@ -42,37 +43,87 @@
     )
 
 
-def gather_kernel(x_ref, g_ref, xo_ref, go_ref, send, recv):
+def gather_kernel(x_ref, g_ref, wi_hbm, wo_hbm, xo_ref, go_ref, w_ref,
+                  wi, wo, s_in, s_out, send, recv, load):
+    loads = [pltpu.make_async_copy(wi_hbm, wi, load.at[0]),
+             pltpu.make_async_copy(wo_hbm, wo, load.at[1])]
+    for copy in loads:
+        copy.start()
     me = lax.axis_index("mp")
-    peers = [{"mp": lax.rem(me + i, NMP)} for i in range(1, NMP)]
-    signal_all(peers)
-    copies = []
-    for i, peer in enumerate(peers):
-        copies.append(remote(x_ref, xo_ref.at[me], send.at[0, i], recv.at[0, i], peer))
-        copies.append(remote(g_ref, go_ref.at[me], send.at[1, i], recv.at[1, i], peer))
-    for copy in copies:
+    nxt, prv = lax.rem(me + 1, NMP), lax.rem(me + NMP - 1, NMP)
+    ahead, behind = {"mp": nxt}, {"mp": prv}
+    signal_all([ahead, behind])
+    x_ahead = remote(x_ref, xo_ref.at[me], send.at[0], recv.at[0], ahead)
+    g_behind = remote(g_ref, go_ref.at[me], send.at[1], recv.at[1], behind)
+    g_ahead = remote(g_ref, go_ref.at[me], send.at[2], recv.at[2], ahead)
+    x_behind = remote(x_ref, xo_ref.at[me], send.at[3], recv.at[3], behind)
+    x_relay = remote(xo_ref.at[prv], xo_ref.at[prv], send.at[4], recv.at[4], ahead)
+    g_relay = remote(go_ref.at[nxt], go_ref.at[nxt], send.at[5], recv.at[5], behind)
+    for copy in (x_ahead, g_behind, g_ahead, x_behind):
         copy.start()
     xo_ref[me] = x_ref[...]
     go_ref[me] = g_ref[...]
-    for copy in copies:
+    for copy in loads:
         copy.wait()
-
-
-def gather_inputs(x_in, grad_out):
+    low = lax.broadcasted_iota(jnp.int32, (8, 2 * BLK), 1) < BLK
+
+    def relayout(r):
+        top = pl.ds(pl.multiple_of(r * KR, KR), KR)
+        for j in range(BLK // 2):
+            lanes = slice(j * 2 * BLK, (j + 1) * 2 * BLK)
+            v = wi[top, lanes].astype(f32)
+            a, b = v[:8], v[8:]
+            s_in[pl.ds(2 * j, 8, stride=BLK), :] = jnp.where(low, a, pltpu.roll(b, BLK, 1))
+            s_in[pl.ds(2 * j + 1, 8, stride=BLK), :] = jnp.where(low, pltpu.roll(a, BLK, 1), b)
+            v = wo[top, lanes].astype(f32)
+            for h in range(2):
+                u = v[h * 8:h * 8 + 8]
+                s_out[pl.ds(h * 8 * BLK + 2 * j, 8, stride=BLK), :] = pltpu.roll(u, BLK, 1)
+                s_out[pl.ds(h * 8 * BLK + 2 * j + 1, 8, stride=BLK), :] = u
+        for k in range(8):
+            turned = s_in[k * BLK:(k + 1) * BLK, :].T
+            for h in range(2):
+                kk = h * 8 + k
+                both = jnp.concatenate([
+                    turned[h * BLK:(h + 1) * BLK],
+                    s_out[kk * BLK:(kk + 1) * BLK, BLK:],
+                ], axis=1)
+                w_ref[pl.ds(pl.multiple_of((r * KR + kk) * BLK, BLK), BLK), :] = both.astype(bf16)
+
+    pl.loop(0, RELAY_AT)(relayout)
+    x_ahead.wait_recv()
+    x_relay.start()
+    g_behind.wait_recv()
+    g_relay.start()
+    pl.loop(RELAY_AT, NRB)(relayout)
+    for copy in (g_ahead, x_behind, x_relay, g_relay):
+        copy.wait_recv()
+    for copy in (x_ahead, g_behind, g_ahead, x_behind, x_relay, g_relay):
+        copy.wait_send()
+
+
+def gather_inputs(x_in, grad_out, w_in, w_out):
     whole = jax.ShapeDtypeStruct((NMP, TOK, x_in.shape[1]), bf16)
     vmem = pl.BlockSpec(memory_space=pltpu.VMEM)
+    hbm = pl.BlockSpec(memory_space=pl.ANY)
     return pl.pallas_call(
         gather_kernel,
-        out_shape=(whole, whole),
-        in_specs=[vmem, vmem],
-        out_specs=(vmem, vmem),
+        out_shape=(whole, whole, jax.ShapeDtypeStruct((NRB * KR * BLK, 2 * BLK), bf16)),
+        in_specs=[vmem, vmem, hbm, hbm],
+        out_specs=(vmem, vmem, vmem),
         scratch_shapes=[
-            pltpu.SemaphoreType.DMA((2, NMP - 1)),
-            pltpu.SemaphoreType.DMA((2, NMP - 1)),
+            pltpu.VMEM(w_in.shape, bf16),
+            pltpu.VMEM(w_out.shape, bf16),
+            pltpu.VMEM((KR * BLK // 2, 2 * BLK), f32),
+            pltpu.VMEM((KR * BLK, 2 * BLK), f32),
+            pltpu.SemaphoreType.DMA((6,)),
+            pltpu.SemaphoreType.DMA((6,)),
+            pltpu.SemaphoreType.DMA((2,)),
         ],
-        compiler_params=pltpu.CompilerParams(collective_id=0, has_side_effects=True),
+        compiler_params=pltpu.CompilerParams(
+            collective_id=0, has_side_effects=True, vmem_limit_bytes=40 << 20),
         name="gather_inputs",
-    )(x_in, grad_out)
+    )(x_in, grad_out, w_in, w_out)
 
 
 def compute_kernel(scale, cols, slots, x_ref, g_ref, gain_ref, w_ref,
@@ -345,11 +396,7 @@
 
 
 def body(x_in, gain, w_in, w_out, grad_out, block_cols, slots):
-    whole_x, whole_grad = gather_inputs(x_in, grad_out)
-    weights = jnp.concatenate([
-        w_in.reshape(-1, BLK, BLK).transpose(0, 2, 1),
-        w_out.reshape(-1, BLK, BLK),
-    ], axis=-1).reshape(-1, 2 * BLK)
+    whole_x, whole_grad, weights = gather_inputs(x_in, grad_out, w_in, w_out)
     outgoing, branch_parts, gn_parts = compute(
         block_cols, slots, whole_x, whole_grad, gain.reshape(NMP, 1, 256), weights)
     owned, branch, grad_normed = reduce_all(outgoing, branch_parts, gn_parts)

time: 105 us -> 91.2 us (0.87)
  local copies, waits for them, and re-layouts: 20.4 us -> 8.94 us
  other arithmetic: 5.98 us -> 0 us
  Pallas kernels: 77.7 us -> 81.2 us
    transpose x1 -> x0, local copies, waits for them, and re-layouts: 8.05 us -> none  [body(): w_in.reshape(-1, BLK, BLK).transpose(0, 2, 1)]
    concatenate x1 -> x0, local copies, waits for them, and re-layouts: 6.92 us -> none  [body(): jnp.concatenate([w_in.reshape(-1, BLK, BLK).transpose(0, 2, 1), w_out.res...]
    concatenate x1 -> x0, other arithmetic: 5.98 us -> none  [body(): jnp.concatenate([w_in.reshape(-1, BLK, BLK).transpose(0, 2, 1), w_out.res...]
    pallas_call x1, Pallas kernels: 14.1 us -> 19.5 us  [gather_inputs(): pl.pallas_call(gather_kernel, out_shape=(whole, whole, jax.ShapeDtypeStru...]
    unnamed x13 -> x18, local copies, waits for them, and re-layouts: 4.56 us -> 8.07 us
    pallas_call x1, Pallas kernels: 45.6 us -> 43.7 us  [reduce_all(): pl.pallas_call(reduce_kernel, out_shape=(jax.ShapeDtypeStruct((TOK, 128),...]
where the time goes in v1:
time: 91.2 us; the launch traced here: 90.8 us
  Pallas kernels  81.2 us (89%)
  local copies, waits for them, and re-layouts  8.94 us (10%)
    pallas_call x1, Pallas kernels, reduce_all(): pl.pallas_call(reduce_kernel, out_shape=(jax.ShapeDtypeStruct((TOK, 128),...  43.7 us
    pallas_call x1, Pallas kernels, gather_inputs(): pl.pallas_call(gather_kernel, out_shape=(whole, whole, jax.ShapeDtypeStru...  19.5 us
    pallas_call x1, Pallas kernels, compute(): pl.pallas_call(functools.partial(compute_kernel, scale), out_shape=(jax.S...  18 us
    unnamed x18, local copies, waits for them, and re-layouts  8.07 us

profile of v1, /device:TPU:8, one launch (start us, length us, event | category | flops | bytes accessed | tf_op | source)
XLA Modules:
  0.0 90.8 jit_solution(5102410314524879678)
XLA Ops:
  0.6 0.0 copy-start.6
  0.6 0.0 copy-start.1
  0.7 1.6 %copy-done.1 = bf16[256,4096]{1,0:T(8,128)(2,1)S(1)} copy-done((bf16[256,4096]{1,0:T(8,128)(2,1)S(1)}, bf16[256,4096]{1,0:T(8,128)(2,1)}, u32[]{:S(2)}) %copy-start.1) | copy-done | bytes 2097176
  2.2 0.0 copy-start.2
  2.2 1.6 %copy-done.2 = bf16[256,4096]{1,0:T(8,128)(2,1)S(1)} copy-done((bf16[256,4096]{1,0:T(8,128)(2,1)S(1)}, bf16[256,4096]{1,0:T(8,128)(2,1)}, u32[]{:S(2)}) %copy-start.2) | copy-done | bytes 2097176
  3.8 0.0 copy-start.3
  3.8 0.8 copy-done.3
  4.7 0.0 copy-start.4
  4.7 0.8 copy-done.4
  5.5 0.0 copy-start.5
  5.5 0.0 copy-start.7
  5.5 19.5 %gather_inputs.1 = (bf16[4,128,256]{2,1,0:T(8,128)(2,1)S(1)}, bf16[4,128,256]{2,1,0:T(8,128)(2,1)S(1)}, bf16[16384,128]{1,0:T(8,128)(2,1)S(1)}) custom-call(bf16[128,256]{1,0:T(8,128)(2,1)S(1)} %copy-done.3, bf16[128,256]{1,0:T(8,128)(2,1)S(1)} %copy-done.4, bf16[256,4096]{1,0:T(8,128)(2,1)S(1)} %copy-done.1, bf16[256,4096]{1,0:T(8,128)(2,1)S(1)} %copy-done.2), custom_call_target="tpu_custom_call" | custom-call | tf_op jit(solution)/shard_map/gather_inputs/pallas_call | solution.py:109
  25.0 0.0 copy-start
  25.0 1.9 %copy-done = bf16[16384,128]{1,0:T(8,128)(2,1)} copy-done((bf16[16384,128]{1,0:T(8,128)(2,1)}, bf16[16384,128]{1,0:T(8,128)(2,1)S(1)}, u32[]{:S(2)}) %copy-start) | copy-done | bytes 4194328
  27.0 0.0 copy-done.6
  27.0 0.0 copy-done.5
  27.0 0.0 copy-done.7
  27.0 18.0 %local_compute.1 = (bf16[512,32,128]{2,1,0:T(8,128)(2,1)S(1)}, bf16[4,128,256]{2,1,0:T(8,128)(2,1)S(1)}, bf16[4,128,256]{2,1,0:T(8,128)(2,1)S(1)}) custom-call(s32[1,256]{1,0:T(1,128)S(1)} %copy-done.6, s32[1,256]{1,0:T(1,128)S(1)} %copy-done.7, bf16[4,128,256]{2,1,0:T(8,128)(2,1)S(1)} %get-tuple-element.12.x_ref, ...), custom_call_target="tpu_custom_call" | custom-call | tf_op jit(solution)/shard_map/local_compute/pallas_call | solution.py:217
  45.0 43.7 %reduce_all.1 = (f32[128,128]{1,0:T(8,128)S(1)}, bf16[128,256]{1,0:T(8,128)(2,1)S(1)}, bf16[128,256]{1,0:T(8,128)(2,1)S(1)}) custom-call(bf16[2,16,4,128,128]{4,3,2,1,0:T(8,128)(2,1)S(1)} %bitcast.5, bf16[4,128,256]{2,1,0:T(8,128)(2,1)S(1)} %get-tuple-element.16.br_src, bf16[4,128,256]{2,1,0:T(8,128)(2,1)S(1)} %get-tuple-element.17.gn_src), custom_call_target="tpu_custom_call" | custom-call | tf_op jit(solution)/shard_map/reduce_all/pallas_call | solution.py:372
  88.7 0.1 reshape.20
  88.8 0.7 reshape.21
  89.6 0.6 copy.13
  90.2 0.6 copy.14
  (1 shorter events, 0.0 us)
Async XLA Ops:
  0.6 26.3 %copy-start.6 = (s32[1,256]{1,0:T(1,128)S(1)}, s32[1,256]{1,0:T(1,128)}, u32[]{:S(2)}) copy-start(s32[1,256]{1,0:T(1,128)} %cols.1) | copy-start | bytes 3076
  0.6 1.6 %copy-start.1 = (bf16[256,4096]{1,0:T(8,128)(2,1)S(1)}, bf16[256,4096]{1,0:T(8,128)(2,1)}, u32[]{:S(2)}) copy-start(bf16[256,4096]{1,0:T(8,128)(2,1)} %wi_hbm.1) | copy-start | bytes 6291460
  2.2 1.6 %copy-start.2 = (bf16[256,4096]{1,0:T(8,128)(2,1)S(1)}, bf16[256,4096]{1,0:T(8,128)(2,1)}, u32[]{:S(2)}) copy-start(bf16[256,4096]{1,0:T(8,128)(2,1)} %wo_hbm.1) | copy-start | bytes 6291460
  3.8 0.8 copy-start.3
  4.7 0.8 copy-start.4
  5.5 21.5 %copy-start.5 = (f32[1024]{0:T(1024)S(1)}, f32[1024]{0:T(1024)}, u32[]{:S(2)}) copy-start(f32[1024]{0:T(1024)} %param.8) | copy-start | bytes 12292
  5.5 21.5 %copy-start.7 = (s32[1,256]{1,0:T(1,128)S(1)}, s32[1,256]{1,0:T(1,128)}, u32[]{:S(2)}) copy-start(s32[1,256]{1,0:T(1,128)} %slots.1) | copy-start | bytes 3076
  25.0 1.9 %copy-start = (bf16[16384,128]{1,0:T(8,128)(2,1)}, bf16[16384,128]{1,0:T(8,128)(2,1)S(1)}, u32[]{:S(2)}) copy-start(bf16[16384,128]{1,0:T(8,128)(2,1)S(1)} %get-tuple-element.14.w_ref) | copy-start | bytes 12582916

commit v2 on v1

--- a/solution.py
+++ b/solution.py
@@ -45,11 +45,13 @@
 
 def gather_kernel(x_ref, g_ref, wi_hbm, wo_hbm, xo_ref, go_ref, w_ref,
                   wi, wo, s_in, s_out, send, recv, load):
+    me = lax.axis_index("mp")
     loads = [pltpu.make_async_copy(wi_hbm, wi, load.at[0]),
-             pltpu.make_async_copy(wo_hbm, wo, load.at[1])]
+             pltpu.make_async_copy(wo_hbm, wo, load.at[1]),
+             pltpu.make_async_copy(x_ref, xo_ref.at[me], load.at[2]),
+             pltpu.make_async_copy(g_ref, go_ref.at[me], load.at[3])]
     for copy in loads:
         copy.start()
-    me = lax.axis_index("mp")
     nxt, prv = lax.rem(me + 1, NMP), lax.rem(me + NMP - 1, NMP)
     ahead, behind = {"mp": nxt}, {"mp": prv}
     signal_all([ahead, behind])
@@ -61,11 +63,12 @@
     g_relay = remote(go_ref.at[nxt], go_ref.at[nxt], send.at[5], recv.at[5], behind)
     for copy in (x_ahead, g_behind, g_ahead, x_behind):
         copy.start()
-    xo_ref[me] = x_ref[...]
-    go_ref[me] = g_ref[...]
     for copy in loads:
         copy.wait()
     low = lax.broadcasted_iota(jnp.int32, (8, 2 * BLK), 1) < BLK
+    square = (2 * BLK, 2 * BLK)
+    eye = (lax.broadcasted_iota(jnp.int32, square, 0)
+           == lax.broadcasted_iota(jnp.int32, square, 1)).astype(f32).astype(bf16)
 
     def relayout(r):
         top = pl.ds(pl.multiple_of(r * KR, KR), KR)
@@ -81,7 +84,8 @@
                 s_out[pl.ds(h * 8 * BLK + 2 * j, 8, stride=BLK), :] = pltpu.roll(u, BLK, 1)
                 s_out[pl.ds(h * 8 * BLK + 2 * j + 1, 8, stride=BLK), :] = u
         for k in range(8):
-            turned = s_in[k * BLK:(k + 1) * BLK, :].T
+            turned = lax.dot_general(
+                eye, s_in[k * BLK:(k + 1) * BLK, :].astype(bf16), NT, preferred_element_type=f32)
             for h in range(2):
                 kk = h * 8 + k
                 both = jnp.concatenate([
@@ -105,11 +109,11 @@
 def gather_inputs(x_in, grad_out, w_in, w_out):
     whole = jax.ShapeDtypeStruct((NMP, TOK, x_in.shape[1]), bf16)
     vmem = pl.BlockSpec(memory_space=pltpu.VMEM)
-    hbm = pl.BlockSpec(memory_space=pl.ANY)
+    hbm = pl.BlockSpec(memory_space=pltpu.HBM)
     return pl.pallas_call(
         gather_kernel,
         out_shape=(whole, whole, jax.ShapeDtypeStruct((NRB * KR * BLK, 2 * BLK), bf16)),
-        in_specs=[vmem, vmem, hbm, hbm],
+        in_specs=[hbm, hbm, hbm, hbm],
         out_specs=(vmem, vmem, vmem),
         scratch_shapes=[
             pltpu.VMEM(w_in.shape, bf16),
@@ -118,12 +122,12 @@
             pltpu.VMEM((KR * BLK, 2 * BLK), f32),
             pltpu.SemaphoreType.DMA((6,)),
             pltpu.SemaphoreType.DMA((6,)),
-            pltpu.SemaphoreType.DMA((2,)),
+            pltpu.SemaphoreType.DMA((4,)),
         ],
         compiler_params=pltpu.CompilerParams(
-            collective_id=0, has_side_effects=True, vmem_limit_bytes=40 << 20),
+            collective_id=0, has_side_effects=True, vmem_limit_bytes=16 << 20),
         name="gather_inputs",
-    )(x_in, grad_out, w_in, w_out)
+    )(*(pltpu.with_memory_space_constraint(a, pltpu.HBM) for a in (x_in, grad_out, w_in, w_out)))
 
 
 def compute_kernel(scale, cols, slots, x_ref, g_ref, gain_ref, w_ref,
@@ -231,7 +235,7 @@
             pltpu.VMEM((NRB * BLK, TOK), f32),
             pltpu.VMEM((NRB * BLK, TOK), f32),
         ],
-        compiler_params=pltpu.CompilerParams(vmem_limit_bytes=48 << 20),
+        compiler_params=pltpu.CompilerParams(vmem_limit_bytes=24 << 20),
         name="local_compute",
     )(cols, slots, whole_x, whole_grad, gain, weights)
 
@@ -390,7 +394,7 @@
             dma((2, NMP - 1)), dma((2, NMP - 1)),
         ],
         compiler_params=pltpu.CompilerParams(
-            collective_id=1, has_side_effects=True, vmem_limit_bytes=40 << 20),
+            collective_id=1, has_side_effects=True, vmem_limit_bytes=16 << 20),
         name="reduce_all",
     )(outgoing.reshape(2, NZ, NX, TOK, 128), branch_parts, gn_parts)
 

time: 91.2 us -> 80.4 us (0.88)
  local copies, waits for them, and re-layouts: 8.94 us -> 2.14 us
  Pallas kernels: 81.2 us -> 77.4 us
    unnamed x18 -> x8, local copies, waits for them, and re-layouts: 8.07 us -> 1.27 us
    pallas_call x1, Pallas kernels: 19.5 us -> 16.5 us  [gather_inputs(): pl.pallas_call(gather_kernel, out_shape=(whole, whole, jax.ShapeDtypeStru...]
    pallas_call x1, Pallas kernels: 18 us -> 16.3 us  [compute(): pl.pallas_call(functools.partial(compute_kernel, scale), out_shape=(jax.S...]
where the time goes in v2:
time: 80.4 us; the launch traced here: 80.2 us
  Pallas kernels  77.4 us (96%)
  local copies, waits for them, and re-layouts  2.14 us (3%)
    pallas_call x1, Pallas kernels, reduce_all(): pl.pallas_call(reduce_kernel, out_shape=(jax.ShapeDtypeStruct((TOK, 128),...  44.5 us
    pallas_call x1, Pallas kernels, gather_inputs(): pl.pallas_call(gather_kernel, out_shape=(whole, whole, jax.ShapeDtypeStru...  16.5 us
    pallas_call x1, Pallas kernels, compute(): pl.pallas_call(functools.partial(compute_kernel, scale), out_shape=(jax.S...  16.3 us

profile of v2, /device:TPU:8, one launch (start us, length us, event | category | flops | bytes accessed | tf_op | source)
XLA Modules:
  0.0 80.2 jit_solution(13553968833700725642)
XLA Ops:
  0.6 0.0 copy-start.2
  0.6 0.0 copy-start.1
  0.7 0.0 copy-start
  0.7 16.5 %gather_inputs.1 = (bf16[4,128,256]{2,1,0:T(8,128)(2,1)S(1)}, bf16[4,128,256]{2,1,0:T(8,128)(2,1)S(1)}, bf16[16384,128]{1,0:T(8,128)(2,1)S(1)}) custom-call(bf16[128,256]{1,0:T(8,128)(2,1)} %x_ref.1, bf16[128,256]{1,0:T(8,128)(2,1)} %g_ref.1, bf16[256,4096]{1,0:T(8,128)(2,1)} %wi_hbm.1, bf16[256,4096]{1,0:T(8,128)(2,1)} %wo_hbm.1), custom_call_target="tpu_custom_call" | custom-call | tf_op jit(solution)/shard_map/gather_inputs/pallas_call | solution.py:113
  17.2 0.0 copy-done.2
  17.2 0.0 copy-done.1
  17.2 0.0 copy-done
  17.2 16.3 %local_compute.1 = (bf16[512,32,128]{2,1,0:T(8,128)(2,1)S(1)}, bf16[4,128,256]{2,1,0:T(8,128)(2,1)S(1)}, bf16[4,128,256]{2,1,0:T(8,128)(2,1)S(1)}) custom-call(s32[1,256]{1,0:T(1,128)S(1)} %copy-done.1, s32[1,256]{1,0:T(1,128)S(1)} %copy-done.2, bf16[4,128,256]{2,1,0:T(8,128)(2,1)S(1)} %get-tuple-element.12.x_ref, ...), custom_call_target="tpu_custom_call" | custom-call | tf_op jit(solution)/shard_map/local_compute/pallas_call | solution.py:221
  33.5 44.5 %reduce_all.1 = (f32[128,128]{1,0:T(8,128)S(1)}, bf16[128,256]{1,0:T(8,128)(2,1)S(1)}, bf16[128,256]{1,0:T(8,128)(2,1)S(1)}) custom-call(bf16[2,16,4,128,128]{4,3,2,1,0:T(8,128)(2,1)S(1)} %bitcast.5, bf16[4,128,256]{2,1,0:T(8,128)(2,1)S(1)} %get-tuple-element.16.br_src, bf16[4,128,256]{2,1,0:T(8,128)(2,1)S(1)} %get-tuple-element.17.gn_src), custom_call_target="tpu_custom_call" | custom-call | tf_op jit(solution)/shard_map/reduce_all/pallas_call | solution.py:376
  78.1 0.1 reshape.20
  78.2 0.7 reshape.21
  79.0 0.6 copy.13
  79.6 0.6 copy.14
  (1 shorter events, 0.0 us)
Async XLA Ops:
  0.6 16.6 %copy-start.2 = (s32[1,256]{1,0:T(1,128)S(1)}, s32[1,256]{1,0:T(1,128)}, u32[]{:S(2)}) copy-start(s32[1,256]{1,0:T(1,128)} %slots.1) | copy-start | bytes 3076
  0.6 16.6 %copy-start.1 = (s32[1,256]{1,0:T(1,128)S(1)}, s32[1,256]{1,0:T(1,128)}, u32[]{:S(2)}) copy-start(s32[1,256]{1,0:T(1,128)} %cols.1) | copy-start | bytes 3076
  0.7 16.6 %copy-start = (f32[1024]{0:T(1024)S(1)}, f32[1024]{0:T(1024)}, u32[]{:S(2)}) copy-start(f32[1024]{0:T(1024)} %param.8) | copy-start | bytes 12292

commit v3 on v2

--- a/solution.py
+++ b/solution.py
@@ -18,7 +18,8 @@
 NMP = 4
 FWD = NZ // 2
 BWD = NZ - 1 - FWD
-RELAY_AT = 4
+RELAY_AT = 8
+HALF = 64
 
 norm_eps = 1e-06
 tanh_coef = 0.7978845608028654
@@ -76,22 +77,25 @@
             lanes = slice(j * 2 * BLK, (j + 1) * 2 * BLK)
             v = wi[top, lanes].astype(f32)
             a, b = v[:8], v[8:]
-            s_in[pl.ds(2 * j, 8, stride=BLK), :] = jnp.where(low, a, pltpu.roll(b, BLK, 1))
-            s_in[pl.ds(2 * j + 1, 8, stride=BLK), :] = jnp.where(low, pltpu.roll(a, BLK, 1), b)
+            for par, u in enumerate((jnp.where(low, a, pltpu.roll(b, BLK, 1)),
+                                     jnp.where(low, pltpu.roll(a, BLK, 1), b))):
+                group, row = divmod(2 * j + par, 8)
+                s_in[pl.ds(group * BLK + row, 8, stride=8), :] = u
             v = wo[top, lanes].astype(f32)
             for h in range(2):
-                u = v[h * 8:h * 8 + 8]
-                s_out[pl.ds(h * 8 * BLK + 2 * j, 8, stride=BLK), :] = pltpu.roll(u, BLK, 1)
-                s_out[pl.ds(h * 8 * BLK + 2 * j + 1, 8, stride=BLK), :] = u
+                for par, u in enumerate((pltpu.roll(v[h * 8:h * 8 + 8], BLK, 1), v[h * 8:h * 8 + 8])):
+                    group, row = divmod(2 * j + par, 8)
+                    s_out[pl.ds((h * 8 + group) * BLK + row, 8, stride=8), :] = u
         for k in range(8):
-            turned = lax.dot_general(
-                eye, s_in[k * BLK:(k + 1) * BLK, :].astype(bf16), NT, preferred_element_type=f32)
+            block = jnp.concatenate(
+                [s_in[g * BLK + k * 8:g * BLK + k * 8 + 8, :] for g in range(8)], axis=0)
+            turned = lax.dot_general(eye, block.astype(bf16), NT, preferred_element_type=f32)
             for h in range(2):
                 kk = h * 8 + k
-                both = jnp.concatenate([
-                    turned[h * BLK:(h + 1) * BLK],
-                    s_out[kk * BLK:(kk + 1) * BLK, BLK:],
-                ], axis=1)
+                lower = jnp.concatenate([
+                    s_out[(h * 8 + g) * BLK + k * 8:(h * 8 + g) * BLK + k * 8 + 8, BLK:]
+                    for g in range(8)], axis=0)
+                both = jnp.concatenate([turned[h * BLK:(h + 1) * BLK], lower], axis=1)
                 w_ref[pl.ds(pl.multiple_of((r * KR + kk) * BLK, BLK), BLK), :] = both.astype(bf16)
 
     pl.loop(0, RELAY_AT)(relayout)
@@ -241,8 +245,10 @@
 
 
 def reduce_kernel(src, br_src, gn_src, owned, br_out, gn_out,
-                  from_core, f_send, f_recv, b_send, b_recv, x_send, x_recv, m_recv,
-                  core_ss, core_rs, f_ss, f_rs, b_ss, b_rs, x_ss, x_rs, m_ss, m_rs):
+                  from_core, fa_send, fa_recv, ba_send, ba_recv, bx_send, bx_recv,
+                  fb_send, fb_recv, bb_send, bb_recv, x_send, x_recv, m_recv,
+                  core_ss, core_rs, fa_ss, fa_rs, ba_ss, ba_rs, bx_ss, bx_rs,
+                  fb_ss, fb_rs, bb_ss, bb_rs, x_ss, x_rs, m_ss, m_rs):
     dp, mp = lax.axis_index("dp"), lax.axis_index("mp")
     core = lax.rem(dp, 2)
     z = lax.rem(dp // 2, NZ)
@@ -264,20 +270,14 @@
     def b_dest(s):
         return lax.rem(z + NZ - BWD + s, NZ)
 
-    core_copies = {}
-
     def core_copy(d):
         return remote(src.at[1 - core, d], from_core.at[d], core_ss.at[d], core_rs.at[d], partner)
 
     @pl.loop(0, FWD)
     def _(s):
         core_copy(f_dest(s)).start()
-
-        @pl.when(s < BWD)
-        def _():
-            core_copy(b_dest(s)).start()
-
-    core_copy(z).start()
+        core_copy(b_dest(s)).start()
+
     mp_copies = []
     for i, peer in enumerate(m_peers):
         to = lax.rem(mp + i + 1, NMP)
@@ -286,42 +286,92 @@
     for copy in mp_copies:
         copy.start()
 
-    def f_copy(s, q):
-        return remote(f_send.at[s, q], f_recv.at[s, q], f_ss.at[s, q], f_rs.at[s, q], ahead)
-
-    def b_copy(s, q):
-        return remote(b_send.at[s, q], b_recv.at[s, q], b_ss.at[s, q], b_rs.at[s, q], behind)
-
-    def pair(d, q):
-        return src[core, d, q].astype(f32) + from_core[d, q].astype(f32)
-
-    core_copy(f_dest(0)).wait_recv()
-    for q in range(NX):
-        f_send[0, q] = pair(f_dest(0), q).astype(bf16)
-        f_copy(0, q).start()
-    core_copy(b_dest(0)).wait_recv()
-    for q in range(NX):
-        b_send[0, q] = pair(b_dest(0), q).astype(bf16)
-        b_copy(0, q).start()
-
-    @pl.loop(1, FWD)
+    def fa_copy(s, q):
+        return remote(fa_send.at[s, q], fa_recv.at[s, q], fa_ss.at[s, q], fa_rs.at[s, q], ahead)
+
+    def ba_copy(s, q):
+        return remote(ba_send.at[s, q], ba_recv.at[s, q], ba_ss.at[s, q], ba_rs.at[s, q], behind)
+
+    def bx_copy(s, i):
+        return remote(bx_send.at[s, i], bx_recv.at[s, i], bx_ss.at[s, i], bx_rs.at[s, i], x_peers[i])
+
+    def fb_copy(s):
+        return remote(fb_send.at[s], fb_recv.at[s], fb_ss.at[s], fb_rs.at[s], ahead)
+
+    def bb_copy(s):
+        return remote(bb_send.at[s], bb_recv.at[s], bb_ss.at[s], bb_rs.at[s], behind)
+
+    def upper(d, q):
+        return src[core, d, q, :HALF].astype(f32) + from_core[d, q, :HALF].astype(f32)
+
+    def lower(d, q):
+        return src[core, d, q, HALF:].astype(f32) + from_core[d, q, HALF:].astype(f32)
+
+    def a_step(s, first=False, back=True):
+        for q in range(2):
+            if not first:
+                fa_copy(s - 1, q).wait_recv()
+            for c in range(2):
+                total = upper(f_dest(s), 2 * q + c)
+                if not first:
+                    total += fa_recv[s - 1, q, c].astype(f32)
+                fa_send[s, q, c] = total.astype(bf16)
+            fa_copy(s, q).start()
+            if back:
+                if not first:
+                    ba_copy(s - 1, q).wait_recv()
+                for c in range(2):
+                    total = upper(b_dest(s), 2 * q + c)
+                    if not first:
+                        total += ba_recv[s - 1, q, c].astype(f32)
+                    ba_send[s, q, c] = total.astype(bf16)
+                ba_copy(s, q).start()
+
+    def bx_step(s):
+        core_copy(f_dest(s)).wait_recv()
+        core_copy(b_dest(s)).wait_recv()
+        for i in range(NX - 1):
+            q = lax.rem(x + i + 1, NX)
+            bx_send[s, i, 0] = lower(f_dest(s), q).astype(bf16)
+            bx_send[s, i, 1] = lower(b_dest(s), q).astype(bf16)
+            bx_copy(s, i).start()
+
+    def row_sum(s, d, way):
+        total = lower(d, x)
+        for i in range(NX - 1):
+            total += bx_recv[s, i, way].astype(f32)
+        return total
+
+    def bz_step(s, first=False, back=True):
+        for i in range(NX - 1):
+            bx_copy(s, i).wait_recv()
+        total = row_sum(s, f_dest(s), 0)
+        if not first:
+            fb_copy(s - 1).wait_recv()
+            total += fb_recv[s - 1].astype(f32)
+        fb_send[s] = total.astype(bf16)
+        fb_copy(s).start()
+        if back:
+            total = row_sum(s, b_dest(s), 1)
+            if not first:
+                bb_copy(s - 1).wait_recv()
+                total += bb_recv[s - 1].astype(f32)
+            bb_send[s] = total.astype(bf16)
+            bb_copy(s).start()
+
+    bx_step(0)
+    a_step(0, first=True)
+    bx_step(1)
+    bz_step(0, first=True)
+
+    @pl.loop(1, BWD)
     def _(s):
-        core_copy(f_dest(s)).wait_recv()
-
-        @pl.when(s < BWD)
-        def _():
-            core_copy(b_dest(s)).wait_recv()
-
-        for q in range(NX):
-            f_copy(s - 1, q).wait_recv()
-            f_send[s, q] = (pair(f_dest(s), q) + f_recv[s - 1, q].astype(f32)).astype(bf16)
-            f_copy(s, q).start()
-
-            @pl.when(s < BWD)
-            def _():
-                b_copy(s - 1, q).wait_recv()
-                b_send[s, q] = (pair(b_dest(s), q) + b_recv[s - 1, q].astype(f32)).astype(bf16)
-                b_copy(s, q).start()
+        a_step(s)
+        bx_step(s + 1)
+        bz_step(s)
+
+    a_step(FWD - 1, back=False)
+    bz_step(FWD - 1, back=False)
 
     for o, (out, own_part) in enumerate(((br_out, br_src), (gn_out, gn_src))):
         total = own_part[mp].astype(f32)
@@ -330,14 +380,14 @@
             total += m_recv[o, i].astype(f32)
         out[...] = total.astype(bf16)
 
-    core_copy(z).wait_recv()
-    for q in range(NX):
-        b_copy(BWD - 1, q).wait_recv()
-    for q in range(NX):
-        f_copy(FWD - 1, q).wait_recv()
+    for q in range(2):
+        ba_copy(BWD - 1, q).wait_recv()
+    for q in range(2):
+        fa_copy(FWD - 1, q).wait_recv()
 
     def whole(q):
-        return pair(z, q) + f_recv[FWD - 1, q].astype(f32) + b_recv[BWD - 1, q].astype(f32)
+        return (upper(z, q) + fa_recv[FWD - 1, q // 2, lax.rem(q, 2)].astype(f32)
+                + ba_recv[BWD - 1, q // 2, lax.rem(q, 2)].astype(f32))
 
     x_copies = []
     for i, peer in enumerate(x_peers):
@@ -345,11 +395,16 @@
         copy = remote(x_send.at[i], x_recv.at[i], x_ss.at[i], x_rs.at[i], peer)
         copy.start()
         x_copies.append(copy)
+
+    bb_copy(BWD - 1).wait_recv()
+    fb_copy(FWD - 1).wait_recv()
+    owned[HALF:] = (row_sum(FWD - 1, z, 1) + fb_recv[FWD - 1].astype(f32)
+                    + bb_recv[BWD - 1].astype(f32))
     total = whole(x)
     for i in range(NX - 1):
         x_copies[i].wait_recv()
         total += x_recv[i].astype(f32)
-    owned[...] = total
+    owned[:HALF] = total
 
     for copy in x_copies + mp_copies:
         copy.wait_send()
@@ -360,36 +415,48 @@
 
     @pl.loop(0, FWD)
     def _(s):
-        for q in range(NX):
-            f_copy(s, q).wait_send()
-
-            @pl.when(s < BWD)
-            def _():
-                b_copy(s, q).wait_send()
+        for q in range(2):
+            fa_copy(s, q).wait_send()
+        for i in range(NX - 1):
+            bx_copy(s, i).wait_send()
+        fb_copy(s).wait_send()
+
+    @pl.loop(0, BWD)
+    def _(s):
+        for q in range(2):
+            ba_copy(s, q).wait_send()
+        bb_copy(s).wait_send()
 
 
 def reduce_all(outgoing, branch_parts, gn_parts):
     vmem = pl.BlockSpec(memory_space=pltpu.VMEM)
     dma = pltpu.SemaphoreType.DMA
-    chunk = (NX, TOK, 128)
+    part = (HALF, 2 * BLK)
     feats = jax.ShapeDtypeStruct((TOK, 256), bf16)
+
+    def buf(*lead):
+        return pltpu.VMEM(lead + part, bf16)
+
     return pl.pallas_call(
         reduce_kernel,
         out_shape=(jax.ShapeDtypeStruct((TOK, 128), f32), feats, feats),
         in_specs=[vmem, vmem, vmem],
         out_specs=(vmem, vmem, vmem),
         scratch_shapes=[
-            pltpu.VMEM((NZ,) + chunk, bf16),
-            pltpu.VMEM((FWD,) + chunk, bf16),
-            pltpu.VMEM((FWD,) + chunk, bf16),
-            pltpu.VMEM((BWD,) + chunk, bf16),
-            pltpu.VMEM((BWD,) + chunk, bf16),
-            pltpu.VMEM((NX - 1, TOK, 128), bf16),
-            pltpu.VMEM((NX - 1, TOK, 128), bf16),
+            pltpu.VMEM((NZ, NX, TOK, 128), bf16),
+            buf(FWD, 2, 2), buf(FWD, 2, 2),
+            buf(BWD, 2, 2), buf(BWD, 2, 2),
+            buf(FWD, NX - 1, 2), buf(FWD, NX - 1, 2),
+            buf(FWD), buf(FWD),
+            buf(BWD), buf(BWD),
+            buf(NX - 1), buf(NX - 1),
             pltpu.VMEM((2, NMP - 1, TOK, 256), bf16),
             dma((NZ,)), dma((NZ,)),
-            dma((FWD, NX)), dma((FWD, NX)),
-            dma((BWD, NX)), dma((BWD, NX)),
+            dma((FWD, 2)), dma((FWD, 2)),
+            dma((BWD, 2)), dma((BWD, 2)),
+            dma((FWD, NX - 1)), dma((FWD, NX - 1)),
+            dma((FWD,)), dma((FWD,)),
+            dma((BWD,)), dma((BWD,)),
             dma((NX - 1,)), dma((NX - 1,)),
             dma((2, NMP - 1)), dma((2, NMP - 1)),
         ],

time: 80.4 us -> 76.3 us (0.949)
  the two profiles are of different devices: /device:TPU:8 before, /device:TPU:4 now
where the time goes in v3:
time: 76.3 us; the launch traced here: 76.2 us
  Pallas kernels  73.3 us (96%)
  local copies, waits for them, and re-layouts  2.14 us (3%)
    pallas_call x1, Pallas kernels, reduce_all(): pl.pallas_call(reduce_kernel, out_shape=(jax.ShapeDtypeStruct((TOK, 128),...  45.6 us
    pallas_call x1, Pallas kernels, compute(): pl.pallas_call(functools.partial(compute_kernel, scale), out_shape=(jax.S...  16.3 us
    pallas_call x1, Pallas kernels, gather_inputs(): pl.pallas_call(gather_kernel, out_shape=(whole, whole, jax.ShapeDtypeStru...  11.4 us

profile of v3, /device:TPU:4, one launch (start us, length us, event | category | flops | bytes accessed | tf_op | source)
XLA Modules:
  0.0 76.2 jit_solution(126064849950064671)
XLA Ops:
  0.6 0.0 copy-start.2
  0.6 0.0 copy-start.1
  0.7 0.0 copy-start
  0.7 11.4 %gather_inputs.1 = (bf16[4,128,256]{2,1,0:T(8,128)(2,1)S(1)}, bf16[4,128,256]{2,1,0:T(8,128)(2,1)S(1)}, bf16[16384,128]{1,0:T(8,128)(2,1)S(1)}) custom-call(bf16[128,256]{1,0:T(8,128)(2,1)} %x_ref.1, bf16[128,256]{1,0:T(8,128)(2,1)} %g_ref.1, bf16[256,4096]{1,0:T(8,128)(2,1)} %wi_hbm.1, bf16[256,4096]{1,0:T(8,128)(2,1)} %wo_hbm.1), custom_call_target="tpu_custom_call" | custom-call | tf_op jit(solution)/shard_map/gather_inputs/pallas_call | solution.py:117
  12.1 0.0 copy-done.2
  12.1 0.0 copy-done.1
  12.1 0.0 copy-done
  12.1 16.3 %local_compute.1 = (bf16[512,32,128]{2,1,0:T(8,128)(2,1)S(1)}, bf16[4,128,256]{2,1,0:T(8,128)(2,1)S(1)}, bf16[4,128,256]{2,1,0:T(8,128)(2,1)S(1)}) custom-call(s32[1,256]{1,0:T(1,128)S(1)} %copy-done.1, s32[1,256]{1,0:T(1,128)S(1)} %copy-done.2, bf16[4,128,256]{2,1,0:T(8,128)(2,1)S(1)} %get-tuple-element.12.x_ref, ...), custom_call_target="tpu_custom_call" | custom-call | tf_op jit(solution)/shard_map/local_compute/pallas_call | solution.py:225
  28.4 45.6 %reduce_all.1 = (f32[128,128]{1,0:T(8,128)S(1)}, bf16[128,256]{1,0:T(8,128)(2,1)S(1)}, bf16[128,256]{1,0:T(8,128)(2,1)S(1)}) custom-call(bf16[2,16,4,128,128]{4,3,2,1,0:T(8,128)(2,1)S(1)} %bitcast.5, bf16[4,128,256]{2,1,0:T(8,128)(2,1)S(1)} %get-tuple-element.16.br_src, bf16[4,128,256]{2,1,0:T(8,128)(2,1)S(1)} %get-tuple-element.17.gn_src), custom_call_target="tpu_custom_call" | custom-call | tf_op jit(solution)/shard_map/reduce_all/pallas_call | solution.py:440
  74.0 0.1 reshape.20
  74.2 0.7 reshape.21
  74.9 0.6 copy.13
  75.5 0.6 copy.14
  (1 shorter events, 0.0 us)
Async XLA Ops:
  0.6 11.5 %copy-start.2 = (s32[1,256]{1,0:T(1,128)S(1)}, s32[1,256]{1,0:T(1,128)}, u32[]{:S(2)}) copy-start(s32[1,256]{1,0:T(1,128)} %slots.1) | copy-start | bytes 3076
  0.6 11.5 %copy-start.1 = (s32[1,256]{1,0:T(1,128)S(1)}, s32[1,256]{1,0:T(1,128)}, u32[]{:S(2)}) copy-start(s32[1,256]{1,0:T(1,128)} %cols.1) | copy-start | bytes 3076
  0.7 11.5 %copy-start = (f32[1024]{0:T(1024)S(1)}, f32[1024]{0:T(1024)}, u32[]{:S(2)}) copy-start(f32[1024]{0:T(1024)} %param.8) | copy-start | bytes 12292

commit v4 on v3

--- a/solution.py
+++ b/solution.py
@@ -136,7 +136,7 @@
 
 def compute_kernel(scale, cols, slots, x_ref, g_ref, gain_ref, w_ref,
                    out_ref, branch_ref, gn_ref,
-                   normed, pre, gact, act, gpre, parts, gath, halves, brt, gnt):
+                   normed, pre, gact, act, gpre, brt, gnt):
     squares = jnp.zeros((TOK, 1), f32)
     for p in range(NMP):
         xf = x_ref[p].astype(f32)
@@ -168,22 +168,23 @@
             lanes = slice(q * BLK, (q + 1) * BLK)
             both = stacked(normed[p, :, lanes], g_ref[p, :, lanes])
             rows = pl.ds(pl.multiple_of(r * KR * BLK, KR * BLK), KR * BLK)
-            parts[...] = lax.dot_general(w_ref[rows, :], both, NT, preferred_element_type=f32)
+            parts = lax.dot_general(w_ref[rows, :], both, NT, preferred_element_type=f32)
             for k in range(KR):
                 at = pl.ds(pl.multiple_of(cols[0, r * KR + k] * BLK, BLK), BLK)
                 pre[at, :] += parts[k * BLK:(k + 1) * BLK, :TOK]
                 gact[at, :] += parts[k * BLK:(k + 1) * BLK, TOK:]
 
-    @pl.loop(0, NCB)
+    @pl.loop(0, NCB // 4)
     def _(i):
-        rows = pl.ds(pl.multiple_of(i * BLK, BLK), BLK)
+        rows = pl.ds(pl.multiple_of(i * (4 * BLK), 4 * BLK), 4 * BLK)
         v = pre[rows, :]
         square = v * v
-        th = jnp.tanh(tanh_coef * (v + 0.044715 * (square * v)))
-        half = 0.5 * v
-        act[rows, :] = (half * (1.0 + th)).astype(bf16)
-        inner = tanh_coef * (1.0 + 0.134145 * square)
-        slope = 0.5 * (1.0 + th) + half * (1.0 - th * th) * inner
+        th = jnp.tanh(v * (tanh_coef + (tanh_coef * 0.044715) * square))
+        rise = 0.5 + 0.5 * th
+        value = v * rise
+        act[rows, :] = value.astype(bf16)
+        inner = tanh_coef + (tanh_coef * 0.134145) * square
+        slope = rise + value * (1.0 - th) * inner
         gpre[rows, :] = (gact[rows, :] * slope).astype(bf16)
 
     @pl.loop(0, NMP)
@@ -192,19 +193,17 @@
             r = p * (NRB // NMP) + q
             lanes = slice(q * BLK, (q + 1) * BLK)
             n_r = normed[p, :, lanes]
-            for k in range(KR):
-                at = pl.ds(pl.multiple_of(cols[0, r * KR + k] * BLK, BLK), BLK)
-                block = gpre[at, :]
-                gath[k * BLK:(k + 1) * BLK, :TOK] = block
-                gath[k * BLK:(k + 1) * BLK, TOK:] = act[at, :]
-                halves[k * 32:(k + 1) * 32, :TOK] = block[:32]
-                halves[k * 32:(k + 1) * 32, TOK:] = block[32:]
+            ats = [pl.ds(pl.multiple_of(cols[0, r * KR + k] * BLK, BLK), BLK) for k in range(KR)]
+            gath = jnp.concatenate(
+                [jnp.concatenate([gpre[at, :], act[at, :]], axis=1) for at in ats], axis=0)
+            halves = jnp.concatenate([
+                jnp.concatenate([gpre[at, :][:32], gpre[at, :][32:]], axis=1) for at in ats], axis=0)
             rows = pl.ds(pl.multiple_of(r * KR * BLK, KR * BLK), KR * BLK)
-            sums = lax.dot_general(w_ref[rows, :], gath[...], TN, preferred_element_type=f32)
+            sums = lax.dot_general(w_ref[rows, :], gath, TN, preferred_element_type=f32)
             at = pl.ds(pl.multiple_of(r * BLK, BLK), BLK)
             gnt[at, :] = sums[:BLK, :TOK]
             brt[at, :] = sums[BLK:, TOK:]
-            grads = jnp.dot(halves[...], stacked(n_r, n_r), preferred_element_type=f32)
+            grads = jnp.dot(halves, stacked(n_r, n_r), preferred_element_type=f32)
             grads = (grads * scale).astype(bf16)
             for k in range(KR):
                 s = slots[0, r * KR + k]
@@ -233,9 +232,6 @@
             pltpu.VMEM((NCB * BLK, TOK), f32),
             pltpu.VMEM((NCB * BLK, TOK), bf16),
             pltpu.VMEM((NCB * BLK, TOK), bf16),
-            pltpu.VMEM((KR * BLK, 2 * TOK), f32),
-            pltpu.VMEM((KR * BLK, 2 * TOK), bf16),
-            pltpu.VMEM((KR * BLK // 2, 2 * TOK), bf16),
             pltpu.VMEM((NRB * BLK, TOK), f32),
             pltpu.VMEM((NRB * BLK, TOK), f32),
         ],
@@ -308,23 +304,19 @@
         return src[core, d, q, HALF:].astype(f32) + from_core[d, q, HALF:].astype(f32)
 
     def a_step(s, first=False, back=True):
-        for q in range(2):
+        for q in range(NX):
+            total = upper(f_dest(s), q)
             if not first:
                 fa_copy(s - 1, q).wait_recv()
-            for c in range(2):
-                total = upper(f_dest(s), 2 * q + c)
-                if not first:
-                    total += fa_recv[s - 1, q, c].astype(f32)
-                fa_send[s, q, c] = total.astype(bf16)
+                total += fa_recv[s - 1, q].astype(f32)
+            fa_send[s, q] = total.astype(bf16)
             fa_copy(s, q).start()
             if back:
+                total = upper(b_dest(s), q)
                 if not first:
                     ba_copy(s - 1, q).wait_recv()
-                for c in range(2):
-                    total = upper(b_dest(s), 2 * q + c)
-                    if not first:
-                        total += ba_recv[s - 1, q, c].astype(f32)
-                    ba_send[s, q, c] = total.astype(bf16)
+                    total += ba_recv[s - 1, q].astype(f32)
+                ba_send[s, q] = total.astype(bf16)
                 ba_copy(s, q).start()
 
     def bx_step(s):
@@ -363,13 +355,16 @@
     a_step(0, first=True)
     bx_step(1)
     bz_step(0, first=True)
-
-    @pl.loop(1, BWD)
+    a_step(1)
+    bx_step(2)
+
+    @pl.loop(2, BWD)
     def _(s):
+        bz_step(s - 1)
         a_step(s)
         bx_step(s + 1)
-        bz_step(s)
-
+
+    bz_step(BWD - 1)
     a_step(FWD - 1, back=False)
     bz_step(FWD - 1, back=False)
 
@@ -380,14 +375,14 @@
             total += m_recv[o, i].astype(f32)
         out[...] = total.astype(bf16)
 
-    for q in range(2):
+    for q in range(NX):
         ba_copy(BWD - 1, q).wait_recv()
-    for q in range(2):
+    for q in range(NX):
         fa_copy(FWD - 1, q).wait_recv()
 
     def whole(q):
-        return (upper(z, q) + fa_recv[FWD - 1, q // 2, lax.rem(q, 2)].astype(f32)
-                + ba_recv[BWD - 1, q // 2, lax.rem(q, 2)].astype(f32))
+        return (upper(z, q) + fa_recv[FWD - 1, q].astype(f32)
+                + ba_recv[BWD - 1, q].astype(f32))
 
     x_copies = []
     for i, peer in enumerate(x_peers):
@@ -415,7 +410,7 @@
 
     @pl.loop(0, FWD)
     def _(s):
-        for q in range(2):
+        for q in range(NX):
             fa_copy(s, q).wait_send()
         for i in range(NX - 1):
             bx_copy(s, i).wait_send()
@@ -423,7 +418,7 @@
 
     @pl.loop(0, BWD)
     def _(s):
-        for q in range(2):
+        for q in range(NX):
             ba_copy(s, q).wait_send()
         bb_copy(s).wait_send()
 
@@ -444,16 +439,16 @@
         out_specs=(vmem, vmem, vmem),
         scratch_shapes=[
             pltpu.VMEM((NZ, NX, TOK, 128), bf16),
-            buf(FWD, 2, 2), buf(FWD, 2, 2),
-            buf(BWD, 2, 2), buf(BWD, 2, 2),
+            buf(FWD, NX), buf(FWD, NX),
+            buf(BWD, NX), buf(BWD, NX),
             buf(FWD, NX - 1, 2), buf(FWD, NX - 1, 2),
             buf(FWD), buf(FWD),
             buf(BWD), buf(BWD),
             buf(NX - 1), buf(NX - 1),
             pltpu.VMEM((2, NMP - 1, TOK, 256), bf16),
             dma((NZ,)), dma((NZ,)),
-            dma((FWD, 2)), dma((FWD, 2)),
-            dma((BWD, 2)), dma((BWD, 2)),
+            dma((FWD, NX)), dma((FWD, NX)),
+            dma((BWD, NX)), dma((BWD, NX)),
             dma((FWD, NX - 1)), dma((FWD, NX - 1)),
             dma((FWD,)), dma((FWD,)),
             dma((BWD,)), dma((BWD,)),

time: 76.3 us -> 73.7 us (0.966)
  Pallas kernels: 73.3 us -> 70.6 us
    pallas_call x1, Pallas kernels: 16.3 us -> 14.3 us  [compute(): pl.pallas_call(functools.partial(compute_kernel, scale), out_shape=(jax.S...]
where the time goes in v4:
time: 73.7 us; the launch traced here: 73.5 us
  Pallas kernels  70.6 us (96%)
  local copies, waits for them, and re-layouts  2.14 us (3%)
    pallas_call x1, Pallas kernels, reduce_all(): pl.pallas_call(reduce_kernel, out_shape=(jax.ShapeDtypeStruct((TOK, 128),...  44.9 us
    pallas_call x1, Pallas kernels, compute(): pl.pallas_call(functools.partial(compute_kernel, scale), out_shape=(jax.S...  14.3 us
    pallas_call x1, Pallas kernels, gather_inputs(): pl.pallas_call(gather_kernel, out_shape=(whole, whole, jax.ShapeDtypeStru...  11.4 us

profile of v4, /device:TPU:4, one launch (start us, length us, event | category | flops | bytes accessed | tf_op | source)
XLA Modules:
  0.0 73.5 jit_solution(14962183879807167629)
XLA Ops:
  0.6 0.0 copy-start.2
  0.6 0.0 copy-start.1
  0.7 0.0 copy-start
  0.7 11.4 %gather_inputs.1 = (bf16[4,128,256]{2,1,0:T(8,128)(2,1)S(1)}, bf16[4,128,256]{2,1,0:T(8,128)(2,1)S(1)}, bf16[16384,128]{1,0:T(8,128)(2,1)S(1)}) custom-call(bf16[128,256]{1,0:T(8,128)(2,1)} %x_ref.1, bf16[128,256]{1,0:T(8,128)(2,1)} %g_ref.1, bf16[256,4096]{1,0:T(8,128)(2,1)} %wi_hbm.1, bf16[256,4096]{1,0:T(8,128)(2,1)} %wo_hbm.1), custom_call_target="tpu_custom_call" | custom-call | tf_op jit(solution)/shard_map/gather_inputs/pallas_call | solution.py:117
  12.1 0.0 copy-done.2
  12.1 0.0 copy-done.1
  12.1 0.0 copy-done
  12.1 14.3 %local_compute.1 = (bf16[512,32,128]{2,1,0:T(8,128)(2,1)S(1)}, bf16[4,128,256]{2,1,0:T(8,128)(2,1)S(1)}, bf16[4,128,256]{2,1,0:T(8,128)(2,1)S(1)}) custom-call(s32[1,256]{1,0:T(1,128)S(1)} %copy-done.1, s32[1,256]{1,0:T(1,128)S(1)} %copy-done.2, bf16[4,128,256]{2,1,0:T(8,128)(2,1)S(1)} %get-tuple-element.12.x_ref, ...), custom_call_target="tpu_custom_call" | custom-call | tf_op jit(solution)/shard_map/local_compute/pallas_call | solution.py:224
  26.4 44.9 %reduce_all.1 = (f32[128,128]{1,0:T(8,128)S(1)}, bf16[128,256]{1,0:T(8,128)(2,1)S(1)}, bf16[128,256]{1,0:T(8,128)(2,1)S(1)}) custom-call(bf16[2,16,4,128,128]{4,3,2,1,0:T(8,128)(2,1)S(1)} %bitcast.5, bf16[4,128,256]{2,1,0:T(8,128)(2,1)S(1)} %get-tuple-element.16.br_src, bf16[4,128,256]{2,1,0:T(8,128)(2,1)S(1)} %get-tuple-element.17.gn_src), custom_call_target="tpu_custom_call" | custom-call | tf_op jit(solution)/shard_map/reduce_all/pallas_call | solution.py:435
  71.3 0.1 reshape.20
  71.5 0.7 %reshape.21 = f32[1,4,4096]{2,1,0:T(4,128)} reshape(f32[4,2,32,64]{3,2,1,0:T(8,128)S(1)} %copy.10) | data formatting | bytes 131072 | tf_op jit(solution)/shard_map/reshape | solution.py:469
  72.2 0.6 copy.13
  72.9 0.6 copy.14
  (1 shorter events, 0.0 us)
Async XLA Ops:
  0.6 11.5 %copy-start.2 = (s32[1,256]{1,0:T(1,128)S(1)}, s32[1,256]{1,0:T(1,128)}, u32[]{:S(2)}) copy-start(s32[1,256]{1,0:T(1,128)} %slots.1) | copy-start | bytes 3076
  0.6 11.5 %copy-start.1 = (s32[1,256]{1,0:T(1,128)S(1)}, s32[1,256]{1,0:T(1,128)}, u32[]{:S(2)}) copy-start(s32[1,256]{1,0:T(1,128)} %cols.1) | copy-start | bytes 3076
  0.7 11.5 %copy-start = (f32[1024]{0:T(1024)S(1)}, f32[1024]{0:T(1024)}, u32[]{:S(2)}) copy-start(f32[1024]{0:T(1024)} %param.8) | copy-start | bytes 12292

commit v5 on v4

--- a/solution.py
+++ b/solution.py
@@ -269,18 +269,17 @@
     def core_copy(d):
         return remote(src.at[1 - core, d], from_core.at[d], core_ss.at[d], core_rs.at[d], partner)
 
-    @pl.loop(0, FWD)
-    def _(s):
+    def core_start(s):
         core_copy(f_dest(s)).start()
         core_copy(b_dest(s)).start()
 
-    mp_copies = []
-    for i, peer in enumerate(m_peers):
+    def m_copy(o, i):
         to = lax.rem(mp + i + 1, NMP)
-        mp_copies.append(remote(br_src.at[to], m_recv.at[0, i], m_ss.at[0, i], m_rs.at[0, i], peer))
-        mp_copies.append(remote(gn_src.at[to], m_recv.at[1, i], m_ss.at[1, i], m_rs.at[1, i], peer))
-    for copy in mp_copies:
-        copy.start()
+        part = (br_src, gn_src)[o]
+        return remote(part.at[to], m_recv.at[o, i], m_ss.at[o, i], m_rs.at[o, i], {"mp": to})
+
+    for s in range(3):
+        core_start(s)
 
     def fa_copy(s, q):
         return remote(fa_send.at[s, q], fa_recv.at[s, q], fa_ss.at[s, q], fa_rs.at[s, q], ahead)
@@ -353,27 +352,32 @@
 
     bx_step(0)
     a_step(0, first=True)
+    core_start(3)
     bx_step(1)
     bz_step(0, first=True)
     a_step(1)
+    core_start(4)
     bx_step(2)
 
     @pl.loop(2, BWD)
     def _(s):
         bz_step(s - 1)
         a_step(s)
+
+        @pl.when(s < FWD - 3)
+        def _():
+            core_start(s + 3)
+
         bx_step(s + 1)
+
+        @pl.when(s >= BWD - 3)
+        def _():
+            for o in range(2):
+                m_copy(o, s - (BWD - 3)).start()
 
     bz_step(BWD - 1)
     a_step(FWD - 1, back=False)
     bz_step(FWD - 1, back=False)
-
-    for o, (out, own_part) in enumerate(((br_out, br_src), (gn_out, gn_src))):
-        total = own_part[mp].astype(f32)
-        for i in range(NMP - 1):
-            mp_copies[2 * i + o].wait_recv()
-            total += m_recv[o, i].astype(f32)
-        out[...] = total.astype(bf16)
 
     for q in range(NX):
         ba_copy(BWD - 1, q).wait_recv()
@@ -395,13 +399,20 @@
     fb_copy(FWD - 1).wait_recv()
     owned[HALF:] = (row_sum(FWD - 1, z, 1) + fb_recv[FWD - 1].astype(f32)
                     + bb_recv[BWD - 1].astype(f32))
+    for o, (out, own_part) in enumerate(((br_out, br_src), (gn_out, gn_src))):
+        total = own_part[mp].astype(f32)
+        for i in range(NMP - 1):
+            m_copy(o, i).wait_recv()
+            total += m_recv[o, i].astype(f32)
+        out[...] = total.astype(bf16)
+
     total = whole(x)
     for i in range(NX - 1):
         x_copies[i].wait_recv()
         total += x_recv[i].astype(f32)
     owned[:HALF] = total
 
-    for copy in x_copies + mp_copies:
+    for copy in x_copies + [m_copy(o, i) for o in range(2) for i in range(NMP - 1)]:
         copy.wait_send()
 
     @pl.loop(0, NZ)

time: 73.7 us -> 73.5 us (level)
  no operation moved by 1% of the time
where the time goes in v5:
time: 73.5 us; the launch traced here: 73.3 us
  Pallas kernels  70.5 us (96%)
  local copies, waits for them, and re-layouts  2.14 us (3%)
    pallas_call x1, Pallas kernels, reduce_all(): pl.pallas_call(reduce_kernel, out_shape=(jax.ShapeDtypeStruct((TOK, 128),...  44.8 us
    pallas_call x1, Pallas kernels, compute(): pl.pallas_call(functools.partial(compute_kernel, scale), out_shape=(jax.S...  14.3 us
    pallas_call x1, Pallas kernels, gather_inputs(): pl.pallas_call(gather_kernel, out_shape=(whole, whole, jax.ShapeDtypeStru...  11.4 us

profile of v5, /device:TPU:4, one launch (start us, length us, event | category | flops | bytes accessed | tf_op | source)
XLA Modules:
  0.0 73.3 jit_solution(7410060938810794200)
XLA Ops:
  0.6 0.0 copy-start.2
  0.6 0.0 copy-start.1
  0.7 0.0 copy-start
  0.7 11.4 %gather_inputs.1 = (bf16[4,128,256]{2,1,0:T(8,128)(2,1)S(1)}, bf16[4,128,256]{2,1,0:T(8,128)(2,1)S(1)}, bf16[16384,128]{1,0:T(8,128)(2,1)S(1)}) custom-call(bf16[128,256]{1,0:T(8,128)(2,1)} %x_ref.1, bf16[128,256]{1,0:T(8,128)(2,1)} %g_ref.1, bf16[256,4096]{1,0:T(8,128)(2,1)} %wi_hbm.1, bf16[256,4096]{1,0:T(8,128)(2,1)} %wo_hbm.1), custom_call_target="tpu_custom_call" | custom-call | tf_op jit(solution)/shard_map/gather_inputs/pallas_call | solution.py:117
  12.1 0.0 copy-done.2
  12.1 0.0 copy-done.1
  12.1 0.0 copy-done
  12.1 14.3 %local_compute.1 = (bf16[512,32,128]{2,1,0:T(8,128)(2,1)S(1)}, bf16[4,128,256]{2,1,0:T(8,128)(2,1)S(1)}, bf16[4,128,256]{2,1,0:T(8,128)(2,1)S(1)}) custom-call(s32[1,256]{1,0:T(1,128)S(1)} %copy-done.1, s32[1,256]{1,0:T(1,128)S(1)} %copy-done.2, bf16[4,128,256]{2,1,0:T(8,128)(2,1)S(1)} %get-tuple-element.12.x_ref, ...), custom_call_target="tpu_custom_call" | custom-call | tf_op jit(solution)/shard_map/local_compute/pallas_call | solution.py:224
  26.4 44.8 %reduce_all.1 = (f32[128,128]{1,0:T(8,128)S(1)}, bf16[128,256]{1,0:T(8,128)(2,1)S(1)}, bf16[128,256]{1,0:T(8,128)(2,1)S(1)}) custom-call(bf16[2,16,4,128,128]{4,3,2,1,0:T(8,128)(2,1)S(1)} %bitcast.5, bf16[4,128,256]{2,1,0:T(8,128)(2,1)S(1)} %get-tuple-element.16.br_src, bf16[4,128,256]{2,1,0:T(8,128)(2,1)S(1)} %get-tuple-element.17.gn_src), custom_call_target="tpu_custom_call" | custom-call | tf_op jit(solution)/shard_map/reduce_all/pallas_call | solution.py:446
  71.2 0.1 reshape.20
  71.3 0.7 %reshape.21 = f32[1,4,4096]{2,1,0:T(4,128)} reshape(f32[4,2,32,64]{3,2,1,0:T(8,128)S(1)} %copy.10) | data formatting | bytes 131072 | tf_op jit(solution)/shard_map/reshape | solution.py:480
  72.1 0.6 copy.13
  72.7 0.6 copy.14
  (1 shorter events, 0.0 us)
Async XLA Ops:
  0.6 11.5 %copy-start.2 = (s32[1,256]{1,0:T(1,128)S(1)}, s32[1,256]{1,0:T(1,128)}, u32[]{:S(2)}) copy-start(s32[1,256]{1,0:T(1,128)} %slots.1) | copy-start | bytes 3076
  0.6 11.5 %copy-start.1 = (s32[1,256]{1,0:T(1,128)S(1)}, s32[1,256]{1,0:T(1,128)}, u32[]{:S(2)}) copy-start(s32[1,256]{1,0:T(1,128)} %cols.1) | copy-start | bytes 3076
  0.7 11.5 %copy-start = (f32[1024]{0:T(1024)S(1)}, f32[1024]{0:T(1024)}, u32[]{:S(2)}) copy-start(f32[1024]{0:T(1024)} %param.8) | copy-start | bytes 12292

commit v6 on v5

--- a/solution.py
+++ b/solution.py
@@ -145,13 +145,11 @@
     for p in range(NMP):
         normed[p] = (x_ref[p].astype(f32) * inv_rms * gain_ref[p]).astype(bf16)
 
-    @pl.loop(0, NCB)
+    @pl.loop(0, NCB // 8)
     def _(i):
-        rows = pl.ds(pl.multiple_of(i * BLK, BLK), BLK)
-        pre[rows, :] = jnp.zeros((BLK, TOK), f32)
-        gact[rows, :] = jnp.zeros((BLK, TOK), f32)
-        for j in range(4):
-            out_ref[i * 4 + j] = jnp.zeros((BLK // 2, 2 * BLK), bf16)
+        rows = pl.ds(pl.multiple_of(i * (8 * BLK), 8 * BLK), 8 * BLK)
+        pre[rows, :] = jnp.zeros((8 * BLK, TOK), f32)
+        gact[rows, :] = jnp.zeros((8 * BLK, TOK), f32)
 
     blank = jnp.zeros((TOK, BLK), bf16)
 
@@ -186,6 +184,8 @@
         inner = tanh_coef + (tanh_coef * 0.134145) * square
         slope = rise + value * (1.0 - th) * inner
         gpre[rows, :] = (gact[rows, :] * slope).astype(bf16)
+        for j in range(16):
+            out_ref[i * 16 + j] = jnp.zeros((BLK // 2, 2 * BLK), bf16)
 
     @pl.loop(0, NMP)
     def _(p):

time: 73.5 us -> 73.2 us (level)
  no operation moved by 1% of the time
where the time goes in v6:
time: 73.2 us; the launch traced here: 73 us
  Pallas kernels  70.2 us (96%)
  local copies, waits for them, and re-layouts  2.14 us (3%)
    pallas_call x1, Pallas kernels, reduce_all(): pl.pallas_call(reduce_kernel, out_shape=(jax.ShapeDtypeStruct((TOK, 128),...  44.8 us
    pallas_call x1, Pallas kernels, compute(): pl.pallas_call(functools.partial(compute_kernel, scale), out_shape=(jax.S...  14 us
    pallas_call x1, Pallas kernels, gather_inputs(): pl.pallas_call(gather_kernel, out_shape=(whole, whole, jax.ShapeDtypeStru...  11.4 us

profile of v6, /device:TPU:4, one launch (start us, length us, event | category | flops | bytes accessed | tf_op | source)
XLA Modules:
  0.0 73.0 jit_solution(8650237039540343281)
XLA Ops:
  0.6 0.0 copy-start.2
  0.6 0.0 copy-start.1
  0.7 0.0 copy-start
  0.7 11.4 %gather_inputs.1 = (bf16[4,128,256]{2,1,0:T(8,128)(2,1)S(1)}, bf16[4,128,256]{2,1,0:T(8,128)(2,1)S(1)}, bf16[16384,128]{1,0:T(8,128)(2,1)S(1)}) custom-call(bf16[128,256]{1,0:T(8,128)(2,1)} %x_ref.1, bf16[128,256]{1,0:T(8,128)(2,1)} %g_ref.1, bf16[256,4096]{1,0:T(8,128)(2,1)} %wi_hbm.1, bf16[256,4096]{1,0:T(8,128)(2,1)} %wo_hbm.1), custom_call_target="tpu_custom_call" | custom-call | tf_op jit(solution)/shard_map/gather_inputs/pallas_call | solution.py:117
  12.1 0.0 copy-done.2
  12.1 0.0 copy-done.1
  12.1 0.0 copy-done
  12.1 14.0 %local_compute.1 = (bf16[512,32,128]{2,1,0:T(8,128)(2,1)S(1)}, bf16[4,128,256]{2,1,0:T(8,128)(2,1)S(1)}, bf16[4,128,256]{2,1,0:T(8,128)(2,1)S(1)}) custom-call(s32[1,256]{1,0:T(1,128)S(1)} %copy-done.1, s32[1,256]{1,0:T(1,128)S(1)} %copy-done.2, bf16[4,128,256]{2,1,0:T(8,128)(2,1)S(1)} %get-tuple-element.12.x_ref, ...), custom_call_target="tpu_custom_call" | custom-call | tf_op jit(solution)/shard_map/local_compute/pallas_call | solution.py:224
  26.1 44.8 %reduce_all.1 = (f32[128,128]{1,0:T(8,128)S(1)}, bf16[128,256]{1,0:T(8,128)(2,1)S(1)}, bf16[128,256]{1,0:T(8,128)(2,1)S(1)}) custom-call(bf16[2,16,4,128,128]{4,3,2,1,0:T(8,128)(2,1)S(1)} %bitcast.5, bf16[4,128,256]{2,1,0:T(8,128)(2,1)S(1)} %get-tuple-element.16.br_src, bf16[4,128,256]{2,1,0:T(8,128)(2,1)S(1)} %get-tuple-element.17.gn_src), custom_call_target="tpu_custom_call" | custom-call | tf_op jit(solution)/shard_map/reduce_all/pallas_call | solution.py:446
  70.9 0.1 reshape.20
  71.0 0.7 %reshape.21 = f32[1,4,4096]{2,1,0:T(4,128)} reshape(f32[4,2,32,64]{3,2,1,0:T(8,128)S(1)} %copy.10) | data formatting | bytes 131072 | tf_op jit(solution)/shard_map/reshape | solution.py:480
  71.8 0.6 copy.13
  72.4 0.6 copy.14
  (1 shorter events, 0.0 us)
Async XLA Ops:
  0.6 11.5 %copy-start.2 = (s32[1,256]{1,0:T(1,128)S(1)}, s32[1,256]{1,0:T(1,128)}, u32[]{:S(2)}) copy-start(s32[1,256]{1,0:T(1,128)} %slots.1) | copy-start | bytes 3076
  0.6 11.5 %copy-start.1 = (s32[1,256]{1,0:T(1,128)S(1)}, s32[1,256]{1,0:T(1,128)}, u32[]{:S(2)}) copy-start(s32[1,256]{1,0:T(1,128)} %cols.1) | copy-start | bytes 3076
  0.7 11.5 %copy-start = (f32[1024]{0:T(1024)S(1)}, f32[1024]{0:T(1024)}, u32[]{:S(2)}) copy-start(f32[1024]{0:T(1024)} %param.8) | copy-start | bytes 12292
